TPU v7x, 256 devices: a whole 4x4x8 slice. The times are simulated.
256 devices in a mesh: row: 16 (over z, core), col: 16 (over x, y).
Axes of the slice: x: 4, y: 4, z: 8, core: 2. Of those that a mesh axis runs over, the one named last changes fastest.
Arguments:
- panel: float32 [16384, 128], P(('row', 'col')), as said below
- mobility: float32 [16384, 16384], P('row', 'col'), as said below
Outputs:
- updated: float32 [16384, 16384], P('row', 'col')
- panel_factor: float32 [128, 128], replicated
Inputs may be any that keep to these rules, and one draw needn't show every extreme that they name: Each row and each column of the panel has its own scale. `mobility`: Symmetric.
All inputs are finite; a program needn't handle non-finite values.
Results may differ from a plain program's by a relative error of at most 0.000076.
Values sent between devices are 32-bit elements; how exact they have to be, the bound alone decides.
No kernel may reach another device: no remote copies, remote signals or barrier semaphores. Data moves between devices by JAX's collectives and lax.ppermute only.
A program may use at most 64 MiB of HBM per device.

v0:
```python
import jax
import jax.numpy as jnp
from jax import lax
from jax.sharding import PartitionSpec as P


def spread(shard, axis, root):
    mine = lax.axis_index(axis) == root
    return lax.psum(jnp.where(mine, shard, jnp.zeros_like(shard)), axis)


def product(first_op, second_op):
    return jnp.dot(
        first_op, second_op, precision=lax.Precision.HIGHEST, preferred_element_type=jnp.float32
    )


def product_tn(first_op, second_op):
    return lax.dot_general(
        first_op,
        second_op,
        (((0,), (0,)), ((), ())),
        precision=lax.Precision.HIGHEST,
        preferred_element_type=jnp.float32,
    )


def product_nt(first_op, second_op):
    return lax.dot_general(
        first_op,
        second_op,
        (((1,), (1,)), ((), ())),
        precision=lax.Precision.HIGHEST,
        preferred_element_type=jnp.float32,
    )


def invert_core(core_matrix):
    identity = jnp.eye(core_matrix.shape[0], dtype=jnp.float32)

    def newton_step(index, approx):
        return product(approx, 2.0 * identity - product(core_matrix, approx))

    return lax.fori_loop(0, 12, newton_step, identity)


def correction_columns(block_rows_arr, block_ratio):
    root_index = lax.axis_index("col") * block_ratio + 0
    copies = spread(block_rows_arr, "row", root_index)
    return copies


def on_device(panel, mobility):
    piece_rows = panel.shape[0]
    width_cols = panel.shape[1]
    count_col = lax.axis_size("col")
    count_row = lax.axis_size("row")
    block_ratio = count_row // count_col
    row_index = lax.axis_index("row")
    col_index = lax.axis_index("col")
    block_rows = mobility.shape[0]
    block_cols = mobility.shape[1]
    first_row = (row_index * count_col + col_index) * piece_rows
    positions = first_row + jnp.arange(piece_rows, dtype=jnp.int32)
    selector = (jnp.arange(width_cols, dtype=jnp.int32)[:, None] == positions[None, :]).astype(
        jnp.float32
    )
    gram_term = product_tn(panel, panel)
    top_term = product(selector, panel)
    gram_sum, top_rows = lax.psum((gram_term, top_term), ("row", "col"))
    lower_factor = jnp.linalg.cholesky(gram_sum)
    panel_factor = lower_factor.T
    ortho_piece = jax.scipy.linalg.solve_triangular(lower_factor, panel.T, lower=True).T
    basis_piece = ortho_piece + selector.T
    top_ortho = jax.scipy.linalg.solve_triangular(lower_factor, top_rows.T, lower=True)
    core_matrix = jnp.eye(width_cols, dtype=jnp.float32) + top_ortho
    kernel = invert_core(core_matrix)
    everything = lax.all_gather(basis_piece, ("row", "col"), axis=0, tiled=True)
    basis_rows = lax.dynamic_slice_in_dim(everything, row_index * block_rows, block_rows, 0)
    basis_cols = lax.dynamic_slice_in_dim(everything, col_index * block_cols, block_cols, 0)
    partial_rows = product(mobility, basis_cols)
    spread_rows = product(lax.psum(partial_rows, "col"), kernel)
    inner_sum = lax.psum(product_tn(basis_rows, spread_rows), "row")
    inner = product_tn(kernel, inner_sum)
    correction_rows = spread_rows - 0.5 * product(basis_rows, inner)
    correction_cols = correction_columns(correction_rows, block_ratio)
    left_side = jnp.concatenate([basis_rows, correction_rows], axis=1)
    right_side = jnp.concatenate([correction_cols, basis_cols], axis=1)
    updated = mobility - product_nt(left_side, right_side)
    return (updated, panel_factor)


def solution(mesh):
    in_specs = (P(("row", "col"), None), P("row", "col"))
    out_specs = (P("row", "col"), P())
    return jax.shard_map(
        on_device, mesh=mesh, in_specs=in_specs, out_specs=out_specs, check_vma=False
    )
```

profile of v0, /device:TPU:1, one launch (start us, length us, event | category | flops | bytes accessed | tf_op | source)
XLA Modules:
  0.0 727.7 jit_solution(3753922273948830282)
XLA Ops:
  7.2 0.7 copy-done
  7.9 0.9 fusion.18
  8.8 0.8 fusion.14
  9.7 249.4 %all-reduce.12.cloned.1.call-done = (f32[128,128]{0,1:T(8,128)}, f32[128,128]{1,0:T(8,128)}) async-done(((f32[128,128]{0,1:T(8,128)}, f32[128,128]{1,0:T(8,128)}), (f32[128,128]{0,1:T(8,128)}, f32[128,128]{1,0:T(8,128)})) %all-reduce.12.cloned.1.call-update) | async-done | bytes 131088 | tf_op jit(solution)/shard_map/psum | solution.py:70
  259.1 0.9 copy.5
  260.0 0.9 fusion.12
  260.9 11.7 %cholesky.19 = f32[128,128]{1,0:T(8,128)S(1)} custom-call(f32[128,128]{1,0:T(8,128)S(1)} %fusion.12), custom_call_target="Cholesky" | custom-call | tf_op jit(solution)/shard_map/jit(cholesky)/cholesky | solution.py:71
  273.3 0.7 fusion.15
  273.9 9.8 %custom-call.10 = f32[1,128,128]{1,2,0:T(8,128)S(1)} custom-call(f32[1,128,128]{2,1,0:T(8,128)S(1)} %get-tuple-element.49), custom_call_target="InvertDiagBlocksLowerTriangular" | custom-call | tf_op jit(solution)/shard_map/jit(_solve_triangular)/triangular_solve | solution.py:73
  283.8 0.8 fusion.3
  284.7 1.1 convolution_add_fusion
  285.9 115.3 %all-gather.2.cloned.1.call-done = f32[16384,128]{1,0:T(8,128)} async-done(((f32[64,128]{1,0:T(8,128)}), f32[16384,128]{1,0:T(8,128)}) %all-gather.2.cloned.1.call-update) | async-done | bytes 8388624 | tf_op jit(solution)/shard_map/all_gather | solution.py:78
  401.2 1.3 constant_dynamic-slice_fusion.1
  402.5 7.5 %convolution_bitcast_fusion.1 = f32[1024,128]{0,1:T(8,128)} fusion(f32[1024,128]{1,0:T(8,128)S(1)} %get-tuple-element.47, f32[1024,1024]{1,0:T(8,128)} %param.5), kind=kOutput, calls=%fused_computation.7 | convolution fusion | flops 1610612736 | bytes 5242880 | tf_op jit(solution)/shard_map/dot_general | solution.py:13
  410.2 7.1 while.11
  417.3 83.1 %all-reduce.6.cloned.1.call-done = f32[1024,128]{0,1:T(8,128)} async-done(((f32[1024,128]{0,1:T(8,128)}), f32[1024,128]{0,1:T(8,128)}) %all-reduce.6.cloned.1.call-update) | async-done | bytes 524304 | tf_op jit(solution)/shard_map/psum | solution.py:82
  500.4 1.6 fusion.19
  502.1 1.6 fusion.20
  504.0 99.9 %all-reduce.8.cloned.1.call-done = f32[128,128]{1,0:T(8,128)} async-done(((f32[128,128]{1,0:T(8,128)}), f32[128,128]{1,0:T(8,128)}) %all-reduce.8.cloned.1.call-update) | async-done | bytes 65552 | tf_op jit(solution)/shard_map/psum | solution.py:83
  603.9 1.0 fusion.21
  604.9 1.4 broadcast_select_fusion
  606.3 0.7 copy.9
  607.1 107.4 %all-reduce.10.cloned.1.call-done = f32[1024,128]{1,0:T(8,128)} async-done(((f32[1024,128]{1,0:T(8,128)}), f32[1024,128]{1,0:T(8,128)}) %all-reduce.10.cloned.1.call-update) | async-done | bytes 524304 | tf_op jit(solution)/shard_map/psum | solution.py:9
  714.4 6.7 convolution_subtract_fusion.1
  (53 shorter events, 8.2 us)
Async XLA Ops:
  7.2 0.8 copy-start
  7.2 251.9 %all-reduce.12.cloned.1.call-start = ((), (), s32[]{:S(2)}) async-start(), calls=%async_computation.4 | async-start | bytes 262144 | tf_op jit(solution)/shard_map/psum | solution.py:70
  9.7 391.5 %all-gather.2.cloned.1.call-start = ((), (), s32[]{:S(2)}) async-start(), calls=%async_computation | async-start | bytes 8421376 | tf_op jit(solution)/shard_map/all_gather | solution.py:78
  284.6 215.8 %all-reduce.6.cloned.1.call-start = ((), (), s32[]{:S(2)}) async-start(), calls=%async_computation.1 | async-start | bytes 1048576 | tf_op jit(solution)/shard_map/psum | solution.py:82
  410.0 193.9 %all-reduce.8.cloned.1.call-start = ((), (), s32[]{:S(2)}) async-start(), calls=%async_computation.2 | async-start | bytes 131072 | tf_op jit(solution)/shard_map/psum | solution.py:83
  503.7 210.7 %all-reduce.10.cloned.1.call-start = ((), (), s32[]{:S(2)}) async-start(), calls=%async_computation.3 | async-start | bytes 1048576 | tf_op jit(solution)/shard_map/psum | solution.py:9
Sparse Core Ops, SparseCore 0:
  14.2 244.8 all-reduce.11
  284.7 116.4 all-gather.1
  410.1 90.2 all-reduce.5
  503.8 99.9 all-reduce.7
  606.6 107.7 all-reduce.9
where the time goes:
time: 728 us
  waiting for transfers between devices  655 us (90%)
  matrix products  30.2 us (4%)
  other arithmetic  23.7 us (3%)
  between operations  13.9 us (2%)
    psum x1, waiting for transfers between devices, on_device(): gram_sum, top_rows = lax.psum((gram_term, top_term), ('row', 'col'))  249 us
    all_gather x1, waiting for transfers between devices, on_device(): everything = lax.all_gather(basis_piece, ('row', 'col'), axis=0, tiled=True)  115 us
    psum x1, waiting for transfers between devices, spread(): return lax.psum(jnp.where(mine, shard, jnp.zeros_like(shard)), axis)  107 us
    psum x1, waiting for transfers between devices, on_device(): inner_sum = lax.psum(product_tn(basis_rows, spread_rows), 'row')  99.9 us
    psum x1, waiting for transfers between devices, on_device(): spread_rows = product(lax.psum(partial_rows, 'col'), kernel)  83.1 us
    dot_general x28, matrix products, product(): jnp.dot(first_op, second_op, precision=lax.Precision.HIGHEST, preferred_e...  17.9 us
  transfers between devices with their start and end apart: 5, of which 5 were waited for; matrix products, arithmetic and copies ran while one was open for 1% of the time, Pallas kernels for 0%

commit v1 on v0

--- a/solution.py
+++ b/solution.py
@@ -2,6 +2,13 @@
 import jax.numpy as jnp
 from jax import lax
 from jax.sharding import PartitionSpec as P
+
+
+def swapped_in(x, mesh_axis, dim):
+    size = lax.axis_size(mesh_axis)
+    shards = jnp.stack([x for _ in range(size)])
+    shards = lax.all_to_all(shards, mesh_axis, split_axis=0, concat_axis=0)
+    return jnp.concatenate(shards, axis=dim)
 
 
 def spread(shard, axis, root):
@@ -75,7 +82,7 @@
     top_ortho = jax.scipy.linalg.solve_triangular(lower_factor, top_rows.T, lower=True)
     core_matrix = jnp.eye(width_cols, dtype=jnp.float32) + top_ortho
     kernel = invert_core(core_matrix)
-    everything = lax.all_gather(basis_piece, ("row", "col"), axis=0, tiled=True)
+    everything = swapped_in(basis_piece, ("row", "col"), 0)
     basis_rows = lax.dynamic_slice_in_dim(everything, row_index * block_rows, block_rows, 0)
     basis_cols = lax.dynamic_slice_in_dim(everything, col_index * block_cols, block_cols, 0)
     partial_rows = product(mobility, basis_cols)

time: 728 us -> 811 us (1.11)
  waiting for transfers between devices: 655 us -> 724 us
  starting transfers between devices: 0.39 us -> 10.9 us
    all_to_all x0 -> x1, waiting for transfers between devices: none -> 185 us  [swapped_in(): shards = lax.all_to_all(shards, mesh_axis, split_axis=0, concat_axis=0)]
    all_gather x1 -> x0, waiting for transfers between devices: 115 us -> none  [on_device(): everything = lax.all_gather(basis_piece, ('row', 'col'), axis=0, tiled=True)]
    all_to_all x0 -> x1, starting transfers between devices: none -> 10.6 us  [swapped_in(): shards = lax.all_to_all(shards, mesh_axis, split_axis=0, concat_axis=0)]
where the time goes in v1:
time: 811 us
  waiting for transfers between devices  724 us (89%)
  matrix products  28.8 us (4%)
  other arithmetic  23.7 us (3%)
  between operations  13.9 us (2%)
  starting transfers between devices  10.9 us (1%)
  local copies, waits for them, and re-layouts  8.45 us (1%)
    psum x1, waiting for transfers between devices, on_device(): gram_sum, top_rows = lax.psum((gram_term, top_term), ('row', 'col'))  249 us
    all_to_all x1, waiting for transfers between devices, swapped_in(): shards = lax.all_to_all(shards, mesh_axis, split_axis=0, concat_axis=0)  185 us
    psum x1, waiting for transfers between devices, spread(): return lax.psum(jnp.where(mine, shard, jnp.zeros_like(shard)), axis)  107 us
    psum x1, waiting for transfers between devices, on_device(): inner_sum = lax.psum(product_tn(basis_rows, spread_rows), 'row')  100 us
    psum x1, waiting for transfers between devices, on_device(): spread_rows = product(lax.psum(partial_rows, 'col'), kernel)  83 us
    dot_general x28, matrix products, product(): jnp.dot(first_op, second_op, precision=lax.Precision.HIGHEST, preferred_e...  18 us
  transfers between devices with their start and end apart: 5, of which 5 were waited for; matrix products, arithmetic and copies ran while one was open for 1% of the time, Pallas kernels for 0%

profile of v1, /device:TPU:1, one launch (start us, length us, event | category | flops | bytes accessed | tf_op | source)
XLA Modules:
  0.0 810.6 jit_solution(15237412350434089871)
XLA Ops:
  7.2 0.7 copy-done
  7.9 0.9 fusion.18
  8.8 0.8 fusion.14
  9.7 249.4 %all-reduce.12.cloned.1.call-done = (f32[128,128]{0,1:T(8,128)}, f32[128,128]{1,0:T(8,128)}) async-done(((f32[128,128]{0,1:T(8,128)}, f32[128,128]{1,0:T(8,128)}), (f32[128,128]{0,1:T(8,128)}, f32[128,128]{1,0:T(8,128)})) %all-reduce.12.cloned.1.call-update) | async-done | bytes 131088 | tf_op jit(solution)/shard_map/psum | solution.py:77
  259.1 0.9 copy.10
  260.0 0.9 fusion.12
  260.9 11.7 %cholesky.19 = f32[128,128]{1,0:T(8,128)S(1)} custom-call(f32[128,128]{1,0:T(8,128)S(1)} %fusion.12), custom_call_target="Cholesky" | custom-call | tf_op jit(solution)/shard_map/jit(cholesky)/cholesky | solution.py:78
  273.3 0.7 fusion.15
  273.9 9.8 %custom-call.10 = f32[1,128,128]{1,2,0:T(8,128)S(1)} custom-call(f32[1,128,128]{2,1,0:T(8,128)S(1)} %get-tuple-element.54), custom_call_target="InvertDiagBlocksLowerTriangular" | custom-call | tf_op jit(solution)/shard_map/jit(_solve_triangular)/triangular_solve | solution.py:80
  283.9 4.3 stack.2
  288.2 10.6 %all-to-all-start = ((f32[256,64,128]{2,1,0:T(8,128)}), f32[256,64,128]{2,1,0:T(8,128)}, u32[]{:S(2)}, u32[]{:S(2)}) async-start(f32[256,64,128]{2,1,0:T(8,128)} %stack.2), calls=%async_computation | async-start | bytes 16777216 | tf_op jit(solution)/shard_map/all_to_all | solution.py:10
  299.5 185.0 %all-to-all-done = f32[256,64,128]{2,1,0:T(8,128)} async-done(((f32[256,64,128]{2,1,0:T(8,128)}), f32[256,64,128]{2,1,0:T(8,128)}, u32[]{:S(2)}, u32[]{:S(2)}) %all-to-all-start) | async-done | bytes 8388640 | tf_op jit(solution)/shard_map/all_to_all | solution.py:10
  484.4 1.3 constant_dynamic-slice_fusion.1
  485.7 7.5 convolution_bitcast_fusion.1
  493.2 7.1 while.11
  500.4 83.0 %all-reduce.6.cloned.1.call-done = f32[1024,128]{0,1:T(8,128)} async-done(((f32[1024,128]{0,1:T(8,128)}), f32[1024,128]{0,1:T(8,128)}) %all-reduce.6.cloned.1.call-update) | async-done | bytes 524304 | tf_op jit(solution)/shard_map/psum | solution.py:89
  583.4 1.6 fusion.19
  585.0 1.6 fusion.20
  586.7 100.1 %all-reduce.8.cloned.1.call-done = f32[128,128]{1,0:T(8,128)} async-done(((f32[128,128]{1,0:T(8,128)}), f32[128,128]{1,0:T(8,128)}) %all-reduce.8.cloned.1.call-update) | async-done | bytes 65552 | tf_op jit(solution)/shard_map/psum | solution.py:90
  686.8 1.0 fusion.21
  687.9 1.4 broadcast_select_fusion
  689.4 0.7 copy.14
  690.5 106.9 %all-reduce.10.cloned.1.call-done = f32[1024,128]{0,1:T(8,128)} async-done(((f32[1024,128]{0,1:T(8,128)}), f32[1024,128]{0,1:T(8,128)}) %all-reduce.10.cloned.1.call-update) | async-done | bytes 524304 | tf_op jit(solution)/shard_map/psum | solution.py:16
  797.4 6.7 convolution_subtract_fusion.1
  (56 shorter events, 8.8 us)
Async XLA Ops:
  7.2 0.8 copy-start
  7.2 251.9 %all-reduce.12.cloned.1.call-start = ((), (), s32[]{:S(2)}) async-start(), calls=%async_computation.4 | async-start | bytes 262144 | tf_op jit(solution)/shard_map/psum | solution.py:77
  288.2 11.0 %copy-start.1 = (f32[128,128]{1,0:T(8,128)S(1)}, f32[128,128]{1,0:T(8,128)}, u32[]{:S(2)}) copy-start(f32[128,128]{1,0:T(8,128)} %get-tuple-element.50) | copy-start | bytes 196612
  288.2 196.2 %all-to-all-start = ((f32[256,64,128]{2,1,0:T(8,128)}), f32[256,64,128]{2,1,0:T(8,128)}, u32[]{:S(2)}, u32[]{:S(2)}) async-start(f32[256,64,128]{2,1,0:T(8,128)} %stack.2), calls=%async_computation | async-start | bytes 16777216 | tf_op jit(solution)/shard_map/all_to_all | solution.py:10
  298.8 284.5 %all-reduce.6.cloned.1.call-start = ((), (), s32[]{:S(2)}) async-start(), calls=%async_computation.1 | async-start | bytes 1048576 | tf_op jit(solution)/shard_map/psum | solution.py:89
  493.2 193.6 %all-reduce.8.cloned.1.call-start = ((), (), s32[]{:S(2)}) async-start(), calls=%async_computation.2 | async-start | bytes 131072 | tf_op jit(solution)/shard_map/psum | solution.py:90
  586.7 210.7 %all-reduce.10.cloned.1.call-start = ((), (), s32[]{:S(2)}) async-start(), calls=%async_computation.3 | async-start | bytes 1048576 | tf_op jit(solution)/shard_map/psum | solution.py:16
Sparse Core Ops, SparseCore 0:
  14.2 244.8 all-reduce.11
  493.3 90.0 all-reduce.5
  586.8 100.0 all-reduce.7
  689.6 107.7 all-reduce.9
